TPU v7x, 512 devices: a whole 4x4x16 slice. The times are simulated.
512 devices in a mesh: tile: 64 (over z, y), rx: 8 (over x, core).
Axes of the slice: x: 4, y: 4, z: 16, core: 2. Of those that a mesh axis runs over, the one named last changes fastest.
Arguments:
- h_adjoint: bfloat16 [128, 2, 3, 64, 64, 128], P('rx', None, None, 'tile'), may hold values from -6 to 6
- conductivity: float32 [64, 64, 128], P(None, 'tile'), may hold values from 0.5 to 5
- tx_field: bfloat16 [128, 2, 3, 64, 64, 128], P('rx', None, None, None, 'tile'), may hold values from -6 to 6
- data_weight: float32 [128, 128], P('rx'), may hold values from -1.5 to 1.5
- tow_index: int32 [8, 8, 2], replicated, may hold values from 0 to 15, as said below
- tow_count: int32 [8, 8], replicated, may hold values from 0 to 2, as said below
Outputs:
- jacobian: float32 [128, 64, 64, 128], P('rx', None, 'tile')
Inputs may be any that keep to these rules, and one draw needn't show every extreme that they name: Each block lists consecutive receivers: tow_index[s, d, j] = tow_index[s, d, 0] + j; slots j >= tow_count[s, d] are padding that no output reads. `tow_count`: in every draw some transmitter group has 2 used slots from every receiver group.
All inputs are finite; a program needn't handle non-finite values.
Results may differ from a plain program's by a relative error of at most 0.0041.
Values may be sent and summed in bfloat16 or wider, within the bound.
A program may use at most 128 MiB of HBM per device.

v0:
```python
import jax
import jax.numpy as jnp
from jax import lax
from jax.sharding import PartitionSpec as P


def shifted(value, axis, steps):
    count = lax.axis_size(axis)
    initial, last = (max(0, -steps), min(count, count - steps))
    return lax.ppermute(value, axis, [(source, source + steps) for source in range(initial, last)])


def lagged(values, along):
    along = along % values.ndim
    length = values.shape[along]
    border = jnp.zeros_like(lax.slice_in_dim(values, 0, 1, axis=along))
    return jnp.concatenate(
        [border, lax.slice_in_dim(values, 0, length - 1, axis=along)], axis=along
    )


def curl_average(potential):
    field_x = potential[..., 0, :, :, :]
    field_y = potential[..., 1, :, :, :]
    field_z = potential[..., 2, :, :, :]
    curl_x = field_z - lagged(field_z, -1) - (field_y - lagged(field_y, -2))
    curl_y = field_x - lagged(field_x, -2) - (field_z - lagged(field_z, -3))
    curl_z = field_y - lagged(field_y, -3) - (field_x - lagged(field_x, -1))
    average_x = 0.5 * (curl_x + lagged(curl_x, -3))
    average_y = 0.5 * (curl_y + lagged(curl_y, -1))
    average_z = 0.5 * (curl_z + lagged(curl_z, -2))
    return jnp.stack([average_x, average_y, average_z], axis=-4)


def cell_field(potentials, neighbour, split_axis, sigma):
    extended = jnp.concatenate([neighbour, potentials], axis=split_axis).astype(jnp.float32)
    whole_curl = curl_average(extended)
    interior = lax.slice_in_dim(whole_curl, 1, whole_curl.shape[split_axis], axis=split_axis)
    return (interior / sigma).astype(jnp.bfloat16)


def on_device(h_adjoint, conductivity, tx_field, data_weight, tow_index, tow_count):
    owners = lax.axis_size("rx")
    owner_index = lax.axis_index("rx")
    neighbour = shifted(h_adjoint, "tile", 1)
    sigma_slab = lax.all_to_all(conductivity, "tile", split_axis=0, concat_axis=1, tiled=True)
    slab_fields = cell_field(h_adjoint, neighbour, 3, sigma_slab)
    cell_fields = lax.all_to_all(slab_fields, "tile", split_axis=4, concat_axis=3, tiled=True)
    per_group = cell_fields.shape[0]
    capacity = tow_index.shape[2]
    receivers = per_group * owners
    slot_ids = jnp.arange(capacity, dtype=jnp.int32)
    indices_in = lax.dynamic_index_in_dim(tow_index, owner_index, 1, False)
    counts_in = lax.dynamic_index_in_dim(tow_count, owner_index, 1, False)
    in_use = (slot_ids[None, :] < counts_in[:, None]).astype(jnp.float32)
    own_blocks = lax.dynamic_index_in_dim(tow_index, owner_index, 0, False)
    picked = jnp.take(cell_fields, own_blocks.reshape(-1), axis=0)
    received = lax.all_to_all(picked, "rx", split_axis=0, concat_axis=0, tiled=True)
    target = (jnp.arange(owners, dtype=jnp.int32)[:, None] * per_group + indices_in).reshape(-1)
    select = (target[:, None] == jnp.arange(receivers, dtype=jnp.int32)[None, :]).astype(
        jnp.float32
    )
    select = select * in_use.reshape(-1)[:, None]
    coupling = jnp.dot(
        data_weight, select.T, precision=lax.Precision.HIGHEST, preferred_element_type=jnp.float32
    ).astype(jnp.bfloat16)
    flattened = received.reshape(received.shape[0], -1)
    combined = jnp.dot(coupling, flattened, preferred_element_type=jnp.float32)
    combined = combined.reshape((coupling.shape[0],) + received.shape[1:])
    jacobian = jnp.sum(
        combined[:, 0] * tx_field[:, 0].astype(jnp.float32)
        - combined[:, 1] * tx_field[:, 1].astype(jnp.float32),
        axis=1,
    )
    return jacobian


def solution(mesh):
    placed = (
        P("rx", None, None, "tile", None, None),
        P(None, "tile", None),
        P("rx", None, None, None, "tile", None),
        P("rx", None),
        P(),
        P(),
    )
    return jax.shard_map(
        on_device,
        mesh=mesh,
        in_specs=placed,
        out_specs=P("rx", None, "tile", None),
        check_vma=False,
    )
```

profile of v0, /device:TPU:1, one launch (start us, length us, event | category | flops | bytes accessed | tf_op | source)
XLA Modules:
  0.0 184.0 jit_solution(4696977537697536475)
XLA Ops:
  0.0 0.0 copy-start
  0.0 4.2 %collective-permute-start = (bf16[16,2,3,1,64,128]{5,4,3,2,1,0:T(8,128)(2,1)}, bf16[16,2,3,1,64,128]{5,4,3,2,1,0:T(8,128)(2,1)S(1)}, u32[]{:S(2)}, u32[]{:S(2)}) collective-permute-start(bf16[16,2,3,1,64,128]{5,4,3,2,1,0:T(8,128)(2,1)} %param.6), channel_id=1, source_target_pairs={{0,8},{8,16},{16,24},{24,32},{32,40},{40,48},{48,56},{56,64},{64,7... | collective-permute-start | bytes 4718600 | tf_op jit(solution)/shard_map/ppermute | solution.py:10
  4.3 18.1 %all-to-all-start = ((f32[64,1,128]{2,1,0:T(1,128)}), f32[64,1,128]{2,1,0:T(1,128)S(1)}, u32[]{:S(2)}, u32[]{:S(2)}) async-start(f32[64,1,128]{2,1,0:T(1,128)} %param.7), calls=%async_computation | async-start | bytes 65536 | tf_op jit(solution)/shard_map/all_to_all | solution.py:46
  22.3 12.1 %collective-permute-done = bf16[16,2,3,1,64,128]{5,4,3,2,1,0:T(8,128)(2,1)S(1)} collective-permute-done((bf16[16,2,3,1,64,128]{5,4,3,2,1,0:T(8,128)(2,1)}, bf16[16,2,3,1,64,128]{5,4,3,2,1,0:T(8,128)(2,1)S(1)}, u32[]{:S(2)}, u32[]{:S(2)}) %collective-permute-start) | collective-permute-done | bytes 1572896 | tf_op jit(solution)/shard_map/ppermute | solution.py:10
  34.5 1.8 maximum_convert_fusion
  36.3 1.1 slice_bitcast_fusion.2
  37.4 0.1 slice.77
  37.5 0.1 slice.79
  37.6 2.3 %subtract_subtract_fusion.2 = (f32[16,2,2,64,128]{4,3,2,1,0:T(8,128)S(1)}, f32[16,2,2,64,128]{4,3,2,1,0:T(8,128)S(1)}, f32[16,2,2,64,128]{4,3,2,1,0:T(8,128)S(1)}) fusion(f32[16,2,2,63,128]{4,3,2,1,0:T(8,128)S(1)} %bitcast.64, f32[16,2,2,64,127]{4,3,2,1,0:T(8,128)S(1)} %bitcast.63, f32[16,2,3,2,64,128]{5,4,3,2,1,0:T(8,128)S(1)} %maximum_convert_fusion, ...), kind=kLoop, calls=%fused_computation.14 | loop fusion | flops 4718592 | bytes 22970368 | tf_op jit(solution)/shard_map/sub | solution.py:26
  40.0 0.1 slice.74
  40.1 2.7 %multiply_bitcast_fusion = (f32[16,2,1,2,64,128]{5,4,3,1,0,2:T(8,128)}, f32[16,2,1,2,64,128]{5,4,3,1,0,2:T(8,128)}) fusion(f32[16,2,2,64,128]{4,3,2,1,0:T(8,128)S(1)} %get-tuple-element.6, f32[16,2,2,63,128]{4,3,2,1,0:T(8,128)S(1)} %bitcast.59, f32[16,2,2,64,128]{4,3,2,1,0:T(8,128)S(1)} %get-tuple-element.7, f32[16,2,2,64,127]{4,3,2,1,0:T(8,128)S(1)} %bitcast.60), kind=kLoop, calls=%fused_computation.9 | loop fusion | flops 2097152 | bytes 12533760 | tf_op jit(solution)/shard_map/stack | solution.py:32
  42.8 0.3 multiply_bitcast_fusion.2
  43.1 10.5 %all-to-all-done = f32[64,1,128]{2,1,0:T(1,128)S(1)} async-done(((f32[64,1,128]{2,1,0:T(1,128)}), f32[64,1,128]{2,1,0:T(1,128)S(1)}, u32[]{:S(2)}, u32[]{:S(2)}) %all-to-all-start) | async-done | bytes 32800 | tf_op jit(solution)/shard_map/all_to_all | solution.py:46
  53.6 2.0 %fusion.1 = bf16[16,2,3,1,64,128]{5,4,3,1,0,2:T(8,128)(2,1)S(1)} fusion(f32[16,2,1,2,64,128]{5,4,3,1,0,2:T(8,128)} %get-tuple-element.13, f32[16,2,1,2,64,128]{5,4,3,1,0,2:T(8,128)} %get-tuple-element.14, f32[16,2,1,2,64,128]{5,4,3,1,0,2:T(8,128)S(1)} %multiply_bitcast_fusion.2, f32[64,128]{1,0:T(8,128)S(1)} %bitcast.69), kind=kLoop, calls=%fused_computation.3 | loop fusion | flops 3145728 | bytes 7897088 | tf_op jit(solution)/shard_map/convert_element_type | solution.py:39
  55.7 2.2 %copy.51 = bf16[16,2,3,1,64,128]{5,0,3,2,1,4:T(8,128)(2,1)} copy(bf16[16,2,3,1,64,128]{5,4,3,1,0,2:T(8,128)(2,1)S(1)} %fusion.1) | data formatting | bytes 3145728 | tf_op jit(solution)/shard_map/convert_element_type | solution.py:39
  57.8 13.9 %all-to-all-start.1 = ((bf16[16,2,3,1,64,128]{5,0,3,2,1,4:T(8,128)(2,1)}), bf16[16,2,3,1,64,128]{5,0,3,2,1,4:T(8,128)(2,1)S(1)}, u32[]{:S(2)}, u32[]{:S(2)}) async-start(bf16[16,2,3,1,64,128]{5,0,3,2,1,4:T(8,128)(2,1)} %copy.51), calls=%async_computation.1 | async-start | bytes 3145728 | tf_op jit(solution)/shard_map/all_to_all | solution.py:48
  71.8 0.0 copy-done.4
  71.8 0.1 copy.48
  71.9 0.1 reshape.160
  72.0 0.1 reshape.159
  72.1 71.5 %all-to-all-done.1 = bf16[16,2,3,1,64,128]{5,0,3,2,1,4:T(8,128)(2,1)S(1)} async-done(((bf16[16,2,3,1,64,128]{5,0,3,2,1,4:T(8,128)(2,1)}), bf16[16,2,3,1,64,128]{5,0,3,2,1,4:T(8,128)(2,1)S(1)}, u32[]{:S(2)}, u32[]{:S(2)}) %all-to-all-start.1) | async-done | bytes 1572896 | tf_op jit(solution)/shard_map/all_to_all | solution.py:48
  143.6 0.6 copy.73
  144.2 0.9 gather_fusion
  145.1 0.2 bitcast_select_fusion
  145.3 1.3 copy.54
  146.6 11.3 %all-to-all-start.2 = ((bf16[16,2,3,64,1,128]{5,3,1,2,4,0:T(8,128)(2,1)}), bf16[16,2,3,64,1,128]{5,3,1,2,4,0:T(8,128)(2,1)S(1)}, u32[]{:S(2)}, u32[]{:S(2)}) async-start(bf16[16,2,3,64,1,128]{5,3,1,2,4,0:T(8,128)(2,1)} %copy.54), calls=%async_computation.2 | async-start | bytes 3145728 | tf_op jit(solution)/shard_map/all_to_all | solution.py:58
  157.9 0.3 dynamic-slice_reduce_fusion
  158.2 0.1 squeeze.21
  158.3 0.1 add.64
  158.3 0.1 add.65
  158.4 0.0 copy-done.5
  158.4 0.2 dynamic-slice_reduce_fusion.1
  158.6 0.1 fusion.10
  158.7 0.1 reshape.163
  158.8 0.0 copy-done
  158.8 0.2 fusion.5
  159.0 0.0 copy-done.3
  159.0 1.3 fusion.13
  160.3 18.3 %all-to-all-done.2 = bf16[16,2,3,64,1,128]{5,3,1,2,4,0:T(8,128)(2,1)S(1)} async-done(((bf16[16,2,3,64,1,128]{5,3,1,2,4,0:T(8,128)(2,1)}), bf16[16,2,3,64,1,128]{5,3,1,2,4,0:T(8,128)(2,1)S(1)}, u32[]{:S(2)}, u32[]{:S(2)}) %all-to-all-start.2) | async-done | bytes 1572896 | tf_op jit(solution)/shard_map/all_to_all | solution.py:58
  178.6 0.2 copy.55
  178.8 0.7 reshape.161
  179.5 0.3 copy.67
  179.8 0.0 copy-start.1
  179.8 1.0 convolution_bitcast_fusion
  180.9 0.1 copy-done.1
  181.0 0.2 copy-done.2
  181.2 1.4 fusion.3
  182.6 1.3 copy.60
  (10 shorter events, 0.0 us)
Async XLA Ops:
  0.0 158.8 %copy-start = (f32[16,128]{1,0:T(8,128)S(1)}, f32[16,128]{1,0:T(8,128)}, u32[]{:S(2)}) copy-start(f32[16,128]{1,0:T(8,128)} %param.9) | copy-start | bytes 24580
  0.0 34.5 %collective-permute-start = (bf16[16,2,3,1,64,128]{5,4,3,2,1,0:T(8,128)(2,1)}, bf16[16,2,3,1,64,128]{5,4,3,2,1,0:T(8,128)(2,1)S(1)}, u32[]{:S(2)}, u32[]{:S(2)}) collective-permute-start(bf16[16,2,3,1,64,128]{5,4,3,2,1,0:T(8,128)(2,1)} %param.6), channel_id=1, source_target_pairs={{0,8},{8,16},{16,24},{24,32},{32,40},{40,48},{48,56},{56,64},{64,7... | collective-permute-start | bytes 4718600 | tf_op jit(solution)/shard_map/ppermute | solution.py:10
  4.3 49.4 %all-to-all-start = ((f32[64,1,128]{2,1,0:T(1,128)}), f32[64,1,128]{2,1,0:T(1,128)S(1)}, u32[]{:S(2)}, u32[]{:S(2)}) async-start(f32[64,1,128]{2,1,0:T(1,128)} %param.7), calls=%async_computation | async-start | bytes 65536 | tf_op jit(solution)/shard_map/all_to_all | solution.py:46
  57.8 13.9 %copy-start.4 = (s32[8,8,2]{1,2,0:T(2,128)S(1)}, s32[8,8,2]{1,2,0:T(2,128)}, u32[]{:S(2)}) copy-start(s32[8,8,2]{1,2,0:T(2,128)} %param.10) | copy-start | bytes 1540
  57.8 85.8 %all-to-all-start.1 = ((bf16[16,2,3,1,64,128]{5,0,3,2,1,4:T(8,128)(2,1)}), bf16[16,2,3,1,64,128]{5,0,3,2,1,4:T(8,128)(2,1)S(1)}, u32[]{:S(2)}, u32[]{:S(2)}) async-start(bf16[16,2,3,1,64,128]{5,0,3,2,1,4:T(8,128)(2,1)} %copy.51), calls=%async_computation.1 | async-start | bytes 3145728 | tf_op jit(solution)/shard_map/all_to_all | solution.py:48
  146.6 11.8 %copy-start.5 = (s32[8,8]{1,0:T(8,128)S(1)}, s32[8,8]{1,0:T(8,128)}, u32[]{:S(2)}) copy-start(s32[8,8]{1,0:T(8,128)} %param.11) | copy-start | bytes 772
  146.6 12.4 %copy-start.3 = (bf16[16,2,3,64,1,128]{5,3,4,2,1,0:T(8,128)(2,1)S(1)}, bf16[16,2,3,64,1,128]{5,3,4,2,1,0:T(8,128)(2,1)}, u32[]{:S(2)}) copy-start(bf16[16,2,3,64,1,128]{5,3,4,2,1,0:T(8,128)(2,1)} %param.8) | copy-start | bytes 4718596
  146.6 32.0 %all-to-all-start.2 = ((bf16[16,2,3,64,1,128]{5,3,1,2,4,0:T(8,128)(2,1)}), bf16[16,2,3,64,1,128]{5,3,1,2,4,0:T(8,128)(2,1)S(1)}, u32[]{:S(2)}, u32[]{:S(2)}) async-start(bf16[16,2,3,64,1,128]{5,3,1,2,4,0:T(8,128)(2,1)} %copy.54), calls=%async_computation.2 | async-start | bytes 3145728 | tf_op jit(solution)/shard_map/all_to_all | solution.py:58
  179.8 1.1 copy-start.1
  179.8 1.4 copy-start.2
where the time goes:
time: 184 us
  waiting for transfers between devices  112 us (61%)
  starting transfers between devices  47.5 us (26%)
  local copies, waits for them, and re-layouts  11.5 us (6%)
  other arithmetic  11 us (6%)
    all_to_all x1, waiting for transfers between devices, on_device(): lax.all_to_all(slab_fields, 'tile', split_axis=4, concat_axis=3, tiled=True)  71.5 us
    all_to_all x1, waiting for transfers between devices, on_device(): lax.all_to_all(picked, 'rx', split_axis=0, concat_axis=0, tiled=True)  18.3 us
    all_to_all x1, starting transfers between devices, on_device(): lax.all_to_all(conductivity, 'tile', split_axis=0, concat_axis=1, tiled=T...  18.1 us
    all_to_all x1, starting transfers between devices, on_device(): lax.all_to_all(slab_fields, 'tile', split_axis=4, concat_axis=3, tiled=True)  13.9 us
    ppermute x1, waiting for transfers between devices, shifted(): lax.ppermute(value, axis, [(source, source + steps) for source in range(i...  12.1 us
    all_to_all x1, starting transfers between devices, on_device(): lax.all_to_all(picked, 'rx', split_axis=0, concat_axis=0, tiled=True)  11.3 us
    all_to_all x1, waiting for transfers between devices, on_device(): lax.all_to_all(conductivity, 'tile', split_axis=0, concat_axis=1, tiled=T...  10.5 us
    ppermute x1, starting transfers between devices, shifted(): lax.ppermute(value, axis, [(source, source + steps) for source in range(i...  4.25 us
  transfers between devices with their start and end apart: 4, of which 4 were waited for; matrix products, arithmetic and copies ran while one was open for 6% of the time, Pallas kernels for 0%

commit v1 on v0

v1 whole, which is shorter than its diff:
```python
import functools

import jax
import jax.numpy as jnp
from jax import lax
from jax.experimental import pallas as pl
from jax.experimental.pallas import tpu as pltpu
from jax.sharding import PartitionSpec as P

XG = 8
RU = 4
MESH = pl.DeviceIdType.MESH


def group_order(groups):
    far = groups // 2
    order = [far]
    for step in range(1, groups):
        for offset in (far - step, far + step):
            if 0 < offset < groups and offset not in order:
                order.append(offset)
    if 0 not in order:
        order.append(0)
    return order


def kernel(messages, h_ref, tx_ref, sigma_ref, sel_ref, coef_ref, out_ref,
           halo, sent, arrived, picked, fields, halo_send, halo_recv,
           tile_send, tile_recv, rx_send, rx_recv):
    tiles = lax.axis_size("tile")
    owners = lax.axis_size("rx")
    me = lax.axis_index("tile")
    own = lax.axis_index("rx")
    groups = tiles // XG
    order = group_order(groups)
    my_group = me // XG
    units = h_ref.shape[0]
    after = lax.rem(me + 1, tiles)

    barrier = pltpu.get_barrier_semaphore()

    def greet_tile(step, _):
        peer = lax.rem(me + step, tiles)
        pl.semaphore_signal(barrier, inc=1, device_id={"tile": peer}, device_id_type=MESH)
        return 0

    def greet_rx(step, _):
        peer = lax.rem(own + step, owners)
        pl.semaphore_signal(barrier, inc=1, device_id={"rx": peer}, device_id_type=MESH)
        return 0

    lax.fori_loop(1, tiles, greet_tile, 0)
    lax.fori_loop(1, owners, greet_rx, 0)
    pl.semaphore_wait(barrier, tiles + owners - 2)

    def halo_copy(unit):
        return pltpu.make_async_remote_copy(
            src_ref=h_ref.at[unit, pl.ds(1, 2)], dst_ref=halo.at[unit],
            send_sem=halo_send.at[unit], recv_sem=halo_recv.at[unit],
            device_id={"tile": after}, device_id_type=MESH)

    for unit in range(units):
        halo_copy(unit).start()

    inner = (me > 0).astype(jnp.float32)
    lanes = lax.broadcasted_iota(jnp.int32, (XG, 8, 128), 2)

    def lag_y(value):
        return jnp.where(lanes == 0, 0.0, pltpu.roll(value, 1, 2))

    def curl_block(unit, base):
        hx = h_ref[unit, 0, pl.ds(base, XG + 1)].astype(jnp.float32)
        hy = h_ref[unit, 1, pl.ds(base, XG + 1)].astype(jnp.float32)
        hz = h_ref[unit, 2, pl.ds(base + 1, XG)].astype(jnp.float32)
        py = halo[unit, 0, pl.ds(base, XG + 1)].astype(jnp.float32) * inner
        pz = halo[unit, 1, pl.ds(base + 1, XG)].astype(jnp.float32) * inner
        both_y = hy + py
        both_z = hz + pz
        diff_xy = hy - py
        curl_y = (hx[1:] - hx[:-1]) - (hz - pz)
        sum_x = hx[1:] + hx[:-1]
        average_x = 0.5 * ((both_z - lag_y(both_z)) - (both_y[1:] - both_y[:-1]))
        average_y = 0.5 * (curl_y + lag_y(curl_y))
        average_z = 0.5 * ((diff_xy[1:] + diff_xy[:-1]) - (sum_x - lag_y(sum_x)))
        sent[pl.ds(base, XG), unit, 0] = average_x.astype(jnp.bfloat16)
        sent[pl.ds(base, XG), unit, 1] = average_y.astype(jnp.bfloat16)
        sent[pl.ds(base, XG), unit, 2] = average_z.astype(jnp.bfloat16)

    first = 0
    for number, count in enumerate(messages):
        span = pl.ds(first, count)
        for unit in range(first, first + count):
            halo_copy(unit).wait_recv()
        for offset in order:
            base = lax.rem(my_group + offset, groups) * XG
            for unit in range(first, first + count):
                curl_block(unit, base)

            def send(step, _, base=base, span=span, number=number):
                layer = base + step

                @pl.when(layer != me)
                def _():
                    pltpu.make_async_remote_copy(
                        src_ref=sent.at[layer, span], dst_ref=arrived.at[me, span],
                        send_sem=tile_send.at[number],
                        recv_sem=tile_recv.at[number, my_group],
                        device_id={"tile": layer}, device_id_type=MESH).start()

                @pl.when(layer == me)
                def _():
                    pltpu.make_async_copy(
                        sent.at[layer, span], arrived.at[me, span],
                        tile_recv.at[number, my_group]).start()
                return 0

            lax.fori_loop(0, XG, send, 0)
        first += count

    def collect(offset):
        group = lax.rem(my_group + groups - offset, groups)
        first = 0
        for number, count in enumerate(messages):
            whole = arrived.at[pl.ds(group * XG, XG), pl.ds(first, count)]
            pltpu.make_async_copy(whole, whole, tile_recv.at[number, group]).wait()
            first += count
        for part in range(3):
            block = arrived[pl.ds(group * XG, XG), :, part]
            block = block.reshape(XG * units * 8, 128)
            chosen = jnp.dot(sel_ref[...], block, preferred_element_type=jnp.float32)
            picked[group, :, part] = chosen.astype(jnp.bfloat16).reshape(owners, 4 * XG, 128)
        fields[group, own] = picked[group, own]

        def forward(step, _):
            peer = lax.rem(own + step, owners)
            pltpu.make_async_remote_copy(
                src_ref=picked.at[group, peer], dst_ref=fields.at[group, own],
                send_sem=rx_send, recv_sem=rx_recv.at[group],
                device_id={"rx": peer}, device_id_type=MESH).start()
            return 0

        lax.fori_loop(1, owners, forward, 0)

    def finish(offset):
        group = lax.rem(my_group + groups - offset, groups)
        others = fields.at[group, pl.ds(0, owners - 1)]
        pltpu.make_async_copy(others, others, rx_recv.at[group]).wait()
        total = None
        for part in range(3):
            block = fields[group, :, part].reshape(owners * 4 * XG, 128)
            combined = jnp.dot(coef_ref[...], block, preferred_element_type=jnp.float32)
            term = combined * tx_ref[group, part].astype(jnp.float32)
            total = term if total is None else total + term
        total = total.reshape(XG, 2, out_ref.shape[2], 128)
        value = total[:, 0] - total[:, 1]
        out_ref[group] = value / sigma_ref[group][:, None, :]

    behind = 2 if groups > 2 else 1
    for place, offset in enumerate(order):
        collect(offset)
        if place >= behind:
            finish(order[place - behind])
    for offset in order[len(order) - min(behind, len(order)):]:
        finish(offset)

    for unit in range(units):
        halo_copy(unit).wait_send()
    first = 0
    for number, count in enumerate(messages):
        rest = sent.at[pl.ds(0, tiles - 1), pl.ds(first, count)]
        pltpu.make_async_copy(rest, rest, tile_send.at[number]).wait()
        first += count
    rest = picked.at[:, pl.ds(0, owners - 1)]
    pltpu.make_async_copy(rest, rest, rx_send).wait()


def transfer(h_units, tx_groups, sigma_groups, sel, coef, messages, call_id):
    units = h_units.shape[0]
    groups, _, rows, cells_y = tx_groups.shape
    tiles = groups * XG
    owners = sel.shape[0] // (4 * XG)
    sources = rows // (2 * XG)
    vmem = pl.BlockSpec(memory_space=pltpu.VMEM)
    bf16 = jnp.bfloat16
    return pl.pallas_call(
        functools.partial(kernel, messages),
        out_shape=jax.ShapeDtypeStruct((groups, XG, sources, cells_y), jnp.float32),
        in_specs=[vmem] * 5,
        out_specs=vmem,
        scratch_shapes=[
            pltpu.VMEM((units, 2, tiles + 1, 8, cells_y), bf16),
            pltpu.VMEM((tiles, units, 3, 8, cells_y), bf16),
            pltpu.VMEM((tiles, units, 3, 8, cells_y), bf16),
            pltpu.VMEM((groups, owners, 3, 4 * XG, cells_y), bf16),
            pltpu.VMEM((groups, owners, 3, 4 * XG, cells_y), bf16),
            pltpu.SemaphoreType.DMA((units,)),
            pltpu.SemaphoreType.DMA((units,)),
            pltpu.SemaphoreType.DMA((len(messages),)),
            pltpu.SemaphoreType.DMA((len(messages), groups)),
            pltpu.SemaphoreType.DMA,
            pltpu.SemaphoreType.DMA((groups,)),
        ],
        compiler_params=pltpu.CompilerParams(
            collective_id=call_id, has_side_effects=True, vmem_limit_bytes=40 * 1024 * 1024),
    )(h_units, tx_groups, sigma_groups, sel, coef)


def on_device(h_adjoint, conductivity, tx_field, data_weight, tow_index, tow_count):
    owners = lax.axis_size("rx")
    own = lax.axis_index("rx")
    receivers, parts, axes, _, layers, cells_y = h_adjoint.shape
    sources = tx_field.shape[0]
    capacity = tow_index.shape[2]
    groups = layers // XG
    units = receivers // RU

    h_units = h_adjoint.reshape(units, RU, parts, axes, layers, cells_y)
    h_units = jnp.transpose(h_units, (0, 3, 4, 2, 1, 5))
    h_units = h_units.reshape(units, axes, layers, parts * RU, cells_y)
    h_units = jnp.pad(h_units, ((0, 0), (0, 0), (1, 0), (0, 0), (0, 0)))

    tx_groups = tx_field.reshape(sources, parts, axes, groups, XG, cells_y)
    tx_groups = jnp.transpose(tx_groups, (3, 2, 4, 1, 0, 5))
    tx_groups = tx_groups.reshape(groups, axes, XG * parts * sources, cells_y)
    sigma_groups = conductivity.reshape(groups, XG, cells_y)

    slots = jnp.arange(capacity, dtype=jnp.int32)
    listed = lax.dynamic_index_in_dim(tow_index, own, 0, False)
    same_x = jnp.arange(XG)[:, None] == jnp.arange(XG)[None, :]
    same_part = jnp.arange(parts)[:, None] == jnp.arange(parts)[None, :]
    number = jnp.arange(receivers, dtype=jnp.int32).reshape(units, RU)
    sel = (
        same_x[None, :, None, None, :, None, None, None]
        & same_part[None, None, :, None, None, None, :, None]
        & (listed[:, None, None, :, None, None, None, None]
           == number[None, None, None, None, None, :, None, :])
    )
    sel = sel.astype(jnp.bfloat16).reshape(owners * XG * parts * capacity, XG * units * parts * RU)

    indices_in = lax.dynamic_index_in_dim(tow_index, own, 1, False)
    counts_in = lax.dynamic_index_in_dim(tow_count, own, 1, False)
    in_use = slots[None, :] < counts_in[:, None]
    target = jnp.arange(owners, dtype=jnp.int32)[:, None] * receivers + indices_in
    chosen = (target[:, :, None] == jnp.arange(receivers * owners, dtype=jnp.int32)) & in_use[:, :, None]
    coupling = jnp.sum(
        jnp.where(chosen[None], data_weight[:, None, None, :], 0.0), axis=-1
    ).astype(jnp.bfloat16)
    coef = jnp.where(
        same_x[:, None, None, None, :, None, None]
        & same_part[None, :, None, None, None, :, None],
        coupling[None, None, :, :, None, None, :],
        jnp.zeros((), jnp.bfloat16),
    ).reshape(XG * parts * sources, owners * XG * parts * capacity)

    messages = (1, units - 1)
    rows = transfer(h_units, tx_groups, sigma_groups, sel, coef, messages, 0)
    rows = rows.reshape(layers, sources, cells_y)
    return jnp.transpose(rows, (1, 0, 2))[:, :, None, :]


def solution(mesh):
    placed = (
        P("rx", None, None, "tile", None, None),
        P(None, "tile", None),
        P("rx", None, None, None, "tile", None),
        P("rx", None),
        P(),
        P(),
    )
    return jax.shard_map(
        on_device,
        mesh=mesh,
        in_specs=placed,
        out_specs=P("rx", None, "tile", None),
        check_vma=False,
    )
```

time: 184 us -> 147 us (0.80)
  Pallas kernels: 0 us -> 121 us
  waiting for transfers between devices: 112 us -> 0 us
  starting transfers between devices: 47.5 us -> 0 us
  local copies, waits for them, and re-layouts: 11.5 us -> 15.8 us
  other arithmetic: 11 us -> 8.74 us
    pallas_call x0 -> x1, Pallas kernels: none -> 121 us  [transfer(): pl.pallas_call(functools.partial(kernel, messages), out_shape=jax.ShapeDt...]
    all_to_all x3 -> x0, waiting for transfers between devices: 100 us -> none  [the longest x1 71.5 us: on_device(): lax.all_to_all(slab_fields, 'tile', split_axis=4, concat_axis=3, tiled=True)]
    all_to_all x3 -> x0, starting transfers between devices: 43.3 us -> none  [the longest x1 18.1 us: on_device(): lax.all_to_all(conductivity, 'tile', split_axis=0, concat_axis=1, tiled=T...]
    ppermute x1 -> x0, waiting for transfers between devices: 12.1 us -> none  [shifted(): lax.ppermute(value, axis, [(source, source + steps) for source in range(i...]
    convert_element_type x2, local copies, waits for them, and re-layouts: 2.25 us -> 8.9 us  [the longest x1 8.9 us: on_device(): sel.astype(jnp.bfloat16)]
    ppermute x1 -> x0, starting transfers between devices: 4.25 us -> none  [shifted(): lax.ppermute(value, axis, [(source, source + steps) for source in range(i...]
    another operation x2 -> x1, other arithmetic: 3.05 us -> 0.01 us  [on_device(): number[None, None, None, None, None, :, None, :]]
    convert_element_type x3 -> x1, other arithmetic: 3.91 us -> 6.85 us  [on_device(): sel.astype(jnp.bfloat16)]
  transfers between devices with their start and end apart: 4 -> 0, of which waited for: 4 -> 0; matrix products, arithmetic and copies ran while one was open for 6% -> 0% of each run, Pallas kernels for 0% -> 0%
where the time goes in v1:
time: 147 us; the launch traced here: 146 us
  Pallas kernels  121 us (82%)
  local copies, waits for them, and re-layouts  15.8 us (11%)
  other arithmetic  8.74 us (6%)
    pallas_call x1, Pallas kernels, transfer(): pl.pallas_call(functools.partial(kernel, messages), out_shape=jax.ShapeDt...  121 us
    convert_element_type x1, local copies, waits for them, and re-layouts, on_device(): sel.astype(jnp.bfloat16)  8.9 us
    convert_element_type x1, other arithmetic, on_device(): sel.astype(jnp.bfloat16)  6.85 us

profile of v1, /device:TPU:1, one launch (start us, length us, event | category | flops | bytes accessed | tf_op | source)
XLA Modules:
  0.0 145.5 jit_solution(929048669583271316)
XLA Ops:
  0.0 0.0 copy-start
  0.0 0.7 copy-done
  0.7 0.1 constant_dynamic-slice_fusion
  0.8 0.1 copy.33
  0.9 0.9 dynamic-slice_reduce_fusion
  1.8 0.1 fusion
  1.8 0.8 select_reduce_fusion
  2.7 0.1 copy.34
  2.8 0.1 broadcast_and_fusion
  2.9 0.8 broadcast_select_fusion
  3.7 1.0 select_n.23
  4.7 0.1 copy.36.coef_ref
  4.8 0.1 copy.32
  4.9 0.1 broadcast_compare_fusion
  5.0 0.5 copy.31
  5.5 0.0 copy-start.2
  5.5 6.8 %and_convert_fusion = bf16[8,8,2,2,8,4,2,4]{7,6,5,4,3,2,1,0:T(2,128)(2,1)} fusion(pred[8,2,4,4]{3,2,1,0:T(4,128)(4,1)S(1)} %broadcast_compare_fusion, pred[8,2,8,2]{3,2,1,0:T(8,128)(4,1)S(1)} %copy.31), kind=kLoop, calls=%fused_computation | loop fusion | flops 131072 | bytes 131584 | tf_op jit(solution)/shard_map/convert_element_type | solution.py:238
  12.3 8.9 %reshape.173.sel_ref = bf16[256,256]{1,0:T(8,128)(2,1)S(1)} reshape(bf16[8,8,2,2,8,4,2,4]{7,6,5,4,3,2,1,0:T(2,128)(2,1)} %and_convert_fusion) | data formatting | bytes 262144 | tf_op jit(solution)/shard_map/convert_element_type | solution.py:238
  21.2 0.0 copy-start.3
  21.2 0.0 copy-done.2
  21.2 0.0 copy-start.1
  21.3 1.2 copy.29
  22.5 0.1 pad.4.h_ref
  22.6 0.0 copy-done.3
  22.6 1.0 copy.30
  23.7 0.0 copy-done.1
  23.7 120.9 %shard_map.64 = f32[8,8,16,128]{3,2,1,0:T(8,128)S(1)} custom-call(bf16[4,3,65,8,128]{4,3,2,1,0:T(8,128)(2,1)S(1)} %pad.4.h_ref, bf16[8,3,256,128]{3,2,1,0:T(8,128)(2,1)S(1)} %bitcast.19, f32[8,8,128]{2,1,0:T(8,128)S(1)} %bitcast.21, bf16[256,256]{1,0:T(8,128)(2,1)S(1)} %reshape.173.sel_ref, bf16[256,256]{1,0:T(8,128)(2,1)S(1)} %copy.36.coef_ref), custom_call_target="tpu_custom_call" | custom-call | tf_op jit(solution)/shard_map/pallas_call | solution.py:185
  144.6 1.0 copy.37
  (8 shorter events, 0.1 us)
Async XLA Ops:
  0.0 0.7 copy-start
  5.5 15.8 %copy-start.2 = (bf16[16,2,3,1,64,128]{5,4,3,2,1,0:T(8,128)(2,1)S(1)}, bf16[16,2,3,1,64,128]{5,4,3,2,1,0:T(8,128)(2,1)}, u32[]{:S(2)}) copy-start(bf16[16,2,3,1,64,128]{5,4,3,2,1,0:T(8,128)(2,1)} %param.6) | copy-start | bytes 4718596
  21.2 1.4 copy-start.3
  21.2 2.4 %copy-start.1 = (f32[64,1,128]{2,1,0:T(1,128)S(1)}, f32[64,1,128]{2,1,0:T(1,128)}, u32[]{:S(2)}) copy-start(f32[64,1,128]{2,1,0:T(1,128)} %param.7) | copy-start | bytes 98308

commit v2 on v1

--- a/solution.py
+++ b/solution.py
@@ -9,6 +9,7 @@
 
 XG = 8
 RU = 4
+MESSAGES = {3: (3,), 4: (4,)}
 MESH = pl.DeviceIdType.MESH
 
 
@@ -24,8 +25,51 @@
     return order
 
 
-def kernel(messages, h_ref, tx_ref, sigma_ref, sel_ref, coef_ref, out_ref,
-           halo, sent, arrived, picked, fields, halo_send, halo_recv,
+def prepare_selection(place_ref, sel_ref, units):
+    shape = sel_ref.shape
+    row = lax.broadcasted_iota(jnp.int32, shape, 0)
+    column = lax.broadcasted_iota(jnp.int32, shape, 1)
+    capacity = place_ref.shape[1]
+    slot = (row // (2 * capacity * XG)) * capacity + row % capacity
+    wanted = jnp.zeros(shape, jnp.int32)
+    for owner in range(place_ref.shape[0]):
+        for number in range(capacity):
+            wanted = jnp.where(slot == owner * capacity + number, place_ref[owner, number], wanted)
+    same_x = (row // (2 * capacity)) % XG == column // (8 * units)
+    same_part = (row // capacity) % 2 == (column // RU) % 2
+    receiver = ((column // 8) % units) * RU + column % RU
+    hit = same_x & same_part & (receiver == wanted)
+    sel_ref[...] = jnp.where(hit, 1.0, 0.0).astype(jnp.bfloat16)
+
+
+def prepare_coupling(index_ref, count_ref, weight_ref, coef_ref, own):
+    owners, _, capacity = index_ref.shape
+    sources, receivers = weight_ref.shape
+    rows, columns = coef_ref.shape
+    per_group = receivers // owners
+    shape = (receivers, columns)
+    column = lax.broadcasted_iota(jnp.int32, shape, 1)
+    slot = (column // (2 * capacity * XG)) * capacity + column % capacity
+    target = jnp.full(shape, -1, jnp.int32)
+    for owner in range(owners):
+        for number in range(capacity):
+            used = number < count_ref[owner, own]
+            listed = jnp.where(used, owner * per_group + index_ref[owner, own, number], -1)
+            target = jnp.where(slot == owner * capacity + number, listed, target)
+    hit = lax.broadcasted_iota(jnp.int32, shape, 0) == target
+    chosen = jnp.where(hit, 1.0, 0.0).astype(jnp.bfloat16)
+    weights = jnp.dot(weight_ref[...].astype(jnp.bfloat16), chosen, preferred_element_type=jnp.float32)
+    block = rows // sources
+    weights = jnp.broadcast_to(weights[None], (block, sources, columns)).reshape(rows, columns)
+    row = lax.broadcasted_iota(jnp.int32, (rows, columns), 0)
+    column = lax.broadcasted_iota(jnp.int32, (rows, columns), 1)
+    same_x = row // (2 * sources) == (column // (2 * capacity)) % XG
+    same_part = (row // sources) % 2 == (column // capacity) % 2
+    coef_ref[...] = jnp.where(same_x & same_part, weights, 0.0).astype(jnp.bfloat16)
+
+
+def kernel(messages, place_ref, index_ref, count_ref, h_ref, tx_ref, sigma_ref, weight_ref, out_ref,
+           halo, sent, arrived, picked, fields, sel_ref, coef_ref, halo_send, halo_recv,
            tile_send, tile_recv, rx_send, rx_recv):
     tiles = lax.axis_size("tile")
     owners = lax.axis_size("rx")
@@ -117,6 +161,9 @@
             lax.fori_loop(0, XG, send, 0)
         first += count
 
+    prepare_selection(place_ref, sel_ref, units)
+    prepare_coupling(index_ref, count_ref, weight_ref, coef_ref, own)
+
     def collect(offset):
         group = lax.rem(my_group + groups - offset, groups)
         first = 0
@@ -174,18 +221,19 @@
     pltpu.make_async_copy(rest, rest, rx_send).wait()
 
 
-def transfer(h_units, tx_groups, sigma_groups, sel, coef, messages, call_id):
+def transfer(place, index, count, h_units, tx_groups, sigma_groups, weight, messages, call_id):
     units = h_units.shape[0]
     groups, _, rows, cells_y = tx_groups.shape
     tiles = groups * XG
-    owners = sel.shape[0] // (4 * XG)
+    owners, capacity = place.shape
     sources = rows // (2 * XG)
+    smem = pl.BlockSpec(memory_space=pltpu.SMEM)
     vmem = pl.BlockSpec(memory_space=pltpu.VMEM)
     bf16 = jnp.bfloat16
     return pl.pallas_call(
         functools.partial(kernel, messages),
         out_shape=jax.ShapeDtypeStruct((groups, XG, sources, cells_y), jnp.float32),
-        in_specs=[vmem] * 5,
+        in_specs=[smem] * 3 + [vmem] * 4,
         out_specs=vmem,
         scratch_shapes=[
             pltpu.VMEM((units, 2, tiles + 1, 8, cells_y), bf16),
@@ -193,6 +241,8 @@
             pltpu.VMEM((tiles, units, 3, 8, cells_y), bf16),
             pltpu.VMEM((groups, owners, 3, 4 * XG, cells_y), bf16),
             pltpu.VMEM((groups, owners, 3, 4 * XG, cells_y), bf16),
+            pltpu.VMEM((owners * XG * 2 * capacity, XG * units * 8), bf16),
+            pltpu.VMEM((rows, owners * XG * 2 * capacity), bf16),
             pltpu.SemaphoreType.DMA((units,)),
             pltpu.SemaphoreType.DMA((units,)),
             pltpu.SemaphoreType.DMA((len(messages),)),
@@ -202,58 +252,51 @@
         ],
         compiler_params=pltpu.CompilerParams(
             collective_id=call_id, has_side_effects=True, vmem_limit_bytes=40 * 1024 * 1024),
-    )(h_units, tx_groups, sigma_groups, sel, coef)
+    )(place, index, count, h_units, tx_groups, sigma_groups, weight)
 
 
 def on_device(h_adjoint, conductivity, tx_field, data_weight, tow_index, tow_count):
-    owners = lax.axis_size("rx")
     own = lax.axis_index("rx")
     receivers, parts, axes, _, layers, cells_y = h_adjoint.shape
     sources = tx_field.shape[0]
-    capacity = tow_index.shape[2]
+    owners, _, capacity = tow_index.shape
     groups = layers // XG
-    units = receivers // RU
-
-    h_units = h_adjoint.reshape(units, RU, parts, axes, layers, cells_y)
-    h_units = jnp.transpose(h_units, (0, 3, 4, 2, 1, 5))
-    h_units = h_units.reshape(units, axes, layers, parts * RU, cells_y)
-    h_units = jnp.pad(h_units, ((0, 0), (0, 0), (1, 0), (0, 0), (0, 0)))
 
     tx_groups = tx_field.reshape(sources, parts, axes, groups, XG, cells_y)
     tx_groups = jnp.transpose(tx_groups, (3, 2, 4, 1, 0, 5))
     tx_groups = tx_groups.reshape(groups, axes, XG * parts * sources, cells_y)
     sigma_groups = conductivity.reshape(groups, XG, cells_y)
 
-    slots = jnp.arange(capacity, dtype=jnp.int32)
-    listed = lax.dynamic_index_in_dim(tow_index, own, 0, False)
-    same_x = jnp.arange(XG)[:, None] == jnp.arange(XG)[None, :]
-    same_part = jnp.arange(parts)[:, None] == jnp.arange(parts)[None, :]
-    number = jnp.arange(receivers, dtype=jnp.int32).reshape(units, RU)
-    sel = (
-        same_x[None, :, None, None, :, None, None, None]
-        & same_part[None, None, :, None, None, None, :, None]
-        & (listed[:, None, None, :, None, None, None, None]
-           == number[None, None, None, None, None, :, None, :])
-    )
-    sel = sel.astype(jnp.bfloat16).reshape(owners * XG * parts * capacity, XG * units * parts * RU)
-
-    indices_in = lax.dynamic_index_in_dim(tow_index, own, 1, False)
-    counts_in = lax.dynamic_index_in_dim(tow_count, own, 1, False)
-    in_use = slots[None, :] < counts_in[:, None]
-    target = jnp.arange(owners, dtype=jnp.int32)[:, None] * receivers + indices_in
-    chosen = (target[:, :, None] == jnp.arange(receivers * owners, dtype=jnp.int32)) & in_use[:, :, None]
-    coupling = jnp.sum(
-        jnp.where(chosen[None], data_weight[:, None, None, :], 0.0), axis=-1
-    ).astype(jnp.bfloat16)
-    coef = jnp.where(
-        same_x[:, None, None, None, :, None, None]
-        & same_part[None, :, None, None, None, :, None],
-        coupling[None, None, :, :, None, None, :],
-        jnp.zeros((), jnp.bfloat16),
-    ).reshape(XG * parts * sources, owners * XG * parts * capacity)
-
-    messages = (1, units - 1)
-    rows = transfer(h_units, tx_groups, sigma_groups, sel, coef, messages, 0)
+    number = jnp.arange(receivers, dtype=jnp.int32)
+    used = jnp.arange(capacity, dtype=jnp.int32) < tow_count[:, :, None]
+    slots = jnp.where(used, tow_index, -1).reshape(owners, owners * capacity)
+    listed = jnp.any(slots[:, :, None] == number, axis=1)
+    most = jnp.max(jnp.sum(listed.astype(jnp.int32), axis=1))
+
+    mine = lax.dynamic_index_in_dim(slots, own, 0, False)
+    before = jnp.any(mine[:, None, None] == number[:, None], axis=0) & (number[:, None] < number)
+    rank = jnp.sum(before.astype(jnp.int32), axis=0)
+    place = jnp.sum(jnp.where(mine[:, None] == number, rank, 0), axis=1).reshape(owners, capacity)
+    has = jnp.any(mine[:, None] == number, axis=0)
+
+    def exchange(units, call_id):
+        if units * RU < receivers:
+            order = jnp.arange(units * RU, dtype=jnp.int32)
+            chosen = jnp.sum(jnp.where(has & (rank == order[:, None]), number, 0), axis=1)
+            h_units = jnp.take(h_adjoint, chosen, axis=0, mode="clip")
+            places = place
+        else:
+            h_units = h_adjoint
+            places = lax.dynamic_index_in_dim(tow_index, own, 0, False)
+        h_units = h_units.reshape(units, RU, parts, axes, layers, cells_y)
+        h_units = jnp.transpose(h_units, (0, 3, 4, 2, 1, 5))
+        h_units = h_units.reshape(units, axes, layers, parts * RU, cells_y)
+        h_units = jnp.pad(h_units, ((0, 0), (0, 0), (1, 0), (0, 0), (0, 0)))
+        return transfer(places, tow_index, tow_count, h_units, tx_groups, sigma_groups,
+                        data_weight, MESSAGES[units], call_id)
+
+    few, every = 3, receivers // RU
+    rows = lax.cond(most <= few * RU, lambda: exchange(few, 0), lambda: exchange(every, 1))
     rows = rows.reshape(layers, sources, cells_y)
     return jnp.transpose(rows, (1, 0, 2))[:, :, None, :]
 

time: 147 us -> 113 us (0.77)
  Pallas kernels: 121 us -> 99.2 us
  local copies, waits for them, and re-layouts: 15.8 us -> 9.13 us
  other arithmetic: 8.74 us -> 2.1 us
    pallas_call x1, Pallas kernels: 121 us -> 99.2 us  [transfer(): pl.pallas_call(functools.partial(kernel, messages), out_shape=jax.ShapeDt...]
    convert_element_type x2 -> x0, local copies, waits for them, and re-layouts: 8.9 us -> none  [the longest x1 8.9 us: on_device(): sel.astype(jnp.bfloat16)]
    convert_element_type x1, other arithmetic: 6.85 us -> 0.08 us  [on_device(): rank = jnp.sum(before.astype(jnp.int32), axis=0)]
    cond x0 -> x1, local copies, waits for them, and re-layouts: none -> 2.01 us  [on_device(): lax.cond(most <= few * RU, lambda: exchange(few, 0), lambda: exchange(eve...]
    gather x0 -> x1, local copies, waits for them, and re-layouts: none -> 1.74 us  [exchange(): h_units = jnp.take(h_adjoint, chosen, axis=0, mode='clip')]
    reshape x1, local copies, waits for them, and re-layouts: 1.02 us -> 2.54 us  [on_device(): tx_groups = tx_field.reshape(sources, parts, axes, groups, XG, cells_y)]
where the time goes in v2:
time: 113 us; the launch traced here: 111 us
  Pallas kernels  99.2 us (88%)
  local copies, waits for them, and re-layouts  9.13 us (8%)
  other arithmetic  2.1 us (2%)
    pallas_call x1, Pallas kernels, transfer(): pl.pallas_call(functools.partial(kernel, messages), out_shape=jax.ShapeDt...  99.2 us
    reshape x1, local copies, waits for them, and re-layouts, on_device(): tx_groups = tx_field.reshape(sources, parts, axes, groups, XG, cells_y)  2.54 us

profile of v2, /device:TPU:1, one launch (start us, length us, event | category | flops | bytes accessed | tf_op | source)
XLA Modules:
  0.0 111.4 jit_solution(16687114339252256871)
XLA Ops:
  0.0 0.7 compare_select_fusion
  0.7 0.1 copy.31
  0.8 0.2 dynamic-slice_reduce_fusion
  1.0 0.1 copy.32
  1.1 0.1 fusion.1
  1.2 0.1 convert_reduce_fusion
  1.3 0.6 reduce_max.9
  2.6 0.1 fusion.2
  2.7 0.1 fusion.4
  2.7 0.0 copy-start
  2.7 0.0 copy-start.1
  2.7 0.0 copy-start.2
  2.8 0.0 copy-start.3
  2.8 0.0 copy-start.4
  2.8 2.5 %copy.33 = bf16[16,2,3,8,8,128]{5,0,1,4,2,3:T(8,128)(2,1)S(1)} copy(bf16[16,2,3,8,8,128]{5,4,3,2,1,0:T(8,128)(2,1)} %bitcast.29) | data formatting | bytes 3145728 | tf_op jit(solution)/shard_map/reshape | solution.py:265
  5.3 0.0 copy-done
  5.3 0.0 copy-done.1
  5.3 0.0 copy-done.2
  5.4 0.0 copy-done.3
  5.4 0.0 copy-done.4
  5.4 104.0 %conditional.1 = (f32[8,8,16,128]{3,2,1,0:T(8,128)}) conditional(s32[]{:T(128)} %convert_element_type.14, (s32[]{:T(128)}, s32[8,8,2]{1,2,0:T(2,128)S(1)}, bf16[16,2,3,1,64,128]{5,4,3,2,1,0:T(8,128)(2,1)S(1)}, s32[8,8]{1,0:T(8,128)S(1)}, bf16[8,3,256,128]{3,2,1,0:T(8,128)(2,1)S(1)}, /*index=5*/f32[8,8,128]{2,1,0:T(8,128)S(1)}, ...), branch_computations={%region_4.5_spmd, %region_5.10_spmd} | conditional | flops 3012 | bytes 7104702 | solution.py:299
  5.6 0.1 fusion.5
  5.7 0.1 select_reduce_fusion
  5.8 0.1 select_reduce_fusion.1
  5.9 0.1 reshape.69.place_ref
  6.0 0.1 copy.35.index_ref
  6.1 1.7 %gather_fusion = bf16[12,2,3,64,128]{4,3,2,1,0:T(8,128)(2,1)} fusion(bf16[16,2,3,64,128]{4,3,2,1,0:T(8,128)(2,1)S(1)} %bitcast.26, s32[1024]{0:T(1024)S(1)} %pad_clamp_fusion), kind=kCustom, calls=%fused_computation | custom fusion | bytes 2359344 | tf_op jit(solution)/shard_map/cond/branch_1_fun/jit(_take)/gather | solution.py:286
  7.9 2.2 %copy.30 = bf16[3,4,2,3,64,128]{5,1,2,4,3,0:T(4,128)(2,1)S(1)} copy(bf16[3,4,2,3,64,128]{5,4,3,2,1,0:T(8,128)(2,1)} %bitcast.27) | data formatting | bytes 2359296 | tf_op jit(solution)/shard_map/cond/branch_1_fun/reshape | solution.py:291
  10.1 0.1 pad.7.h_ref
  10.2 99.2 %branch_1_fun.1 = f32[8,8,16,128]{3,2,1,0:T(8,128)} custom-call(s32[8,2]{1,0:T(8,128)S(1)} %reshape.69.place_ref, s32[8,8,2]{2,1,0:T(8,128)S(1)} %copy.35.index_ref, s32[8,8]{1,0:T(8,128)S(1)} %get-tuple-element.68.count_ref, bf16[3,3,65,8,128]{4,3,2,1,0:T(8,128)(2,1)S(1)} %pad.7.h_ref, bf16[8,3,256,128]{3,2,1,0:T(8,128)(2,1)S(1)} %get-tuple-element.71.tx_ref, ...), custom_call_target="tpu_custom_call" | custom-call | tf_op jit(solution)/shard_map/cond/branch_1_fun/pallas_call | solution.py:233
  109.4 2.0 %copy.36 = f32[8,8,16,128]{3,1,0,2:T(8,128)} copy(f32[8,8,16,128]{3,2,1,0:T(8,128)} %get-tuple-element.127) | data formatting | bytes 1048576 | tf_op jit(solution)/shard_map/cond | solution.py:299
  (4 shorter events, 0.0 us)
Async XLA Ops:
  2.7 2.6 %copy-start = (bf16[16,2,3,1,64,128]{5,4,3,2,1,0:T(8,128)(2,1)S(1)}, bf16[16,2,3,1,64,128]{5,4,3,2,1,0:T(8,128)(2,1)}, u32[]{:S(2)}) copy-start(bf16[16,2,3,1,64,128]{5,4,3,2,1,0:T(8,128)(2,1)} %param.8) | copy-start | bytes 4718596
  2.7 2.6 %copy-start.1 = (f32[64,1,128]{2,1,0:T(1,128)S(1)}, f32[64,1,128]{2,1,0:T(1,128)}, u32[]{:S(2)}) copy-start(f32[64,1,128]{2,1,0:T(1,128)} %param.9) | copy-start | bytes 98308
  2.7 2.6 %copy-start.2 = (s32[8,8,2]{1,2,0:T(2,128)S(1)}, s32[8,8,2]{1,2,0:T(2,128)}, u32[]{:S(2)}) copy-start(s32[8,8,2]{1,2,0:T(2,128)} %param.12) | copy-start | bytes 1540
  2.8 2.6 %copy-start.3 = (s32[8,8]{1,0:T(8,128)S(1)}, s32[8,8]{1,0:T(8,128)}, u32[]{:S(2)}) copy-start(s32[8,8]{1,0:T(8,128)} %param.13) | copy-start | bytes 772
  2.8 2.6 %copy-start.4 = (f32[16,128]{1,0:T(8,128)S(1)}, f32[16,128]{1,0:T(8,128)}, u32[]{:S(2)}) copy-start(f32[16,128]{1,0:T(8,128)} %param.11) | copy-start | bytes 24580

commit v3 on v2

--- a/solution.py
+++ b/solution.py
@@ -8,8 +8,9 @@
 from jax.sharding import PartitionSpec as P
 
 XG = 8
-RU = 4
-MESSAGES = {3: (3,), 4: (4,)}
+RU = 2
+ROWS = 2 * RU
+SIZES = (8, 10, 12)
 MESH = pl.DeviceIdType.MESH
 
 
@@ -35,9 +36,9 @@
     for owner in range(place_ref.shape[0]):
         for number in range(capacity):
             wanted = jnp.where(slot == owner * capacity + number, place_ref[owner, number], wanted)
-    same_x = (row // (2 * capacity)) % XG == column // (8 * units)
+    same_x = (row // (2 * capacity)) % XG == column // (ROWS * units)
     same_part = (row // capacity) % 2 == (column // RU) % 2
-    receiver = ((column // 8) % units) * RU + column % RU
+    receiver = ((column // ROWS) % units) * RU + column % RU
     hit = same_x & same_part & (receiver == wanted)
     sel_ref[...] = jnp.where(hit, 1.0, 0.0).astype(jnp.bfloat16)
 
@@ -107,7 +108,7 @@
         halo_copy(unit).start()
 
     inner = (me > 0).astype(jnp.float32)
-    lanes = lax.broadcasted_iota(jnp.int32, (XG, 8, 128), 2)
+    lanes = lax.broadcasted_iota(jnp.int32, (XG, ROWS, 128), 2)
 
     def lag_y(value):
         return jnp.where(lanes == 0, 0.0, pltpu.roll(value, 1, 2))
@@ -173,7 +174,7 @@
             first += count
         for part in range(3):
             block = arrived[pl.ds(group * XG, XG), :, part]
-            block = block.reshape(XG * units * 8, 128)
+            block = block.reshape(XG * units * ROWS, 128)
             chosen = jnp.dot(sel_ref[...], block, preferred_element_type=jnp.float32)
             picked[group, :, part] = chosen.astype(jnp.bfloat16).reshape(owners, 4 * XG, 128)
         fields[group, own] = picked[group, own]
@@ -236,12 +237,12 @@
         in_specs=[smem] * 3 + [vmem] * 4,
         out_specs=vmem,
         scratch_shapes=[
-            pltpu.VMEM((units, 2, tiles + 1, 8, cells_y), bf16),
-            pltpu.VMEM((tiles, units, 3, 8, cells_y), bf16),
-            pltpu.VMEM((tiles, units, 3, 8, cells_y), bf16),
+            pltpu.VMEM((units, 2, tiles + 1, ROWS, cells_y), bf16),
+            pltpu.VMEM((tiles, units, 3, ROWS, cells_y), bf16),
+            pltpu.VMEM((tiles, units, 3, ROWS, cells_y), bf16),
             pltpu.VMEM((groups, owners, 3, 4 * XG, cells_y), bf16),
             pltpu.VMEM((groups, owners, 3, 4 * XG, cells_y), bf16),
-            pltpu.VMEM((owners * XG * 2 * capacity, XG * units * 8), bf16),
+            pltpu.VMEM((owners * XG * 2 * capacity, XG * units * ROWS), bf16),
             pltpu.VMEM((rows, owners * XG * 2 * capacity), bf16),
             pltpu.SemaphoreType.DMA((units,)),
             pltpu.SemaphoreType.DMA((units,)),
@@ -293,10 +294,12 @@
         h_units = h_units.reshape(units, axes, layers, parts * RU, cells_y)
         h_units = jnp.pad(h_units, ((0, 0), (0, 0), (1, 0), (0, 0), (0, 0)))
         return transfer(places, tow_index, tow_count, h_units, tx_groups, sigma_groups,
-                        data_weight, MESSAGES[units], call_id)
-
-    few, every = 3, receivers // RU
-    rows = lax.cond(most <= few * RU, lambda: exchange(few, 0), lambda: exchange(every, 1))
+                        data_weight, (units,), call_id)
+
+    sizes = SIZES + (receivers,)
+    size = sum((most > limit).astype(jnp.int32) for limit in SIZES)
+    rows = lax.switch(size, [
+        functools.partial(exchange, limit // RU, number) for number, limit in enumerate(sizes)])
     rows = rows.reshape(layers, sources, cells_y)
     return jnp.transpose(rows, (1, 0, 2))[:, :, None, :]
 

time: 113 us -> 114 us (level)
  between operations: 0.74 us -> 2.03 us
where the time goes in v3:
time: 114 us; the launch traced here: 112 us
  Pallas kernels  98.5 us (86%)
  local copies, waits for them, and re-layouts  8.75 us (8%)
  other arithmetic  2.1 us (2%)
  between operations  2.03 us (2%)
    pallas_call x1, Pallas kernels, transfer(): pl.pallas_call(functools.partial(kernel, messages), out_shape=jax.ShapeDt...  98.5 us
    reshape x1, local copies, waits for them, and re-layouts, on_device(): tx_groups = tx_field.reshape(sources, parts, axes, groups, XG, cells_y)  2.54 us
    reshape x1, local copies, waits for them, and re-layouts, exchange(): h_units = h_units.reshape(units, RU, parts, axes, layers, cells_y)  2.49 us

profile of v3, /device:TPU:1, one launch (start us, length us, event | category | flops | bytes accessed | tf_op | source)
XLA Modules:
  0.0 112.3 jit_solution(17416322169979128977)
XLA Ops:
  0.0 0.7 compare_select_fusion
  0.7 0.1 copy.41
  0.8 0.2 dynamic-slice_reduce_fusion
  1.0 0.1 copy.42
  1.1 0.1 fusion.3
  1.2 0.1 convert_reduce_fusion
  1.3 0.6 reduce_max.9
  3.9 0.1 fusion.4
  4.0 0.1 fusion.6
  4.0 0.0 copy-start
  4.0 0.0 copy-start.1
  4.0 0.0 copy-start.2
  4.1 0.0 copy-start.3
  4.1 0.0 copy-start.4
  4.1 2.5 %copy.43 = bf16[16,2,3,8,8,128]{5,0,1,4,2,3:T(8,128)(2,1)S(1)} copy(bf16[16,2,3,8,8,128]{5,4,3,2,1,0:T(8,128)(2,1)} %bitcast.47) | data formatting | bytes 3145728 | tf_op jit(solution)/shard_map/reshape | solution.py:266
  6.6 0.0 copy-done
  6.6 0.0 copy-done.1
  6.6 0.0 copy-done.2
  6.7 0.0 copy-done.3
  6.7 0.0 copy-done.4
  6.7 104.6 %conditional.1 = (f32[8,8,16,128]{3,2,1,0:T(8,128)S(1)}) conditional(s32[]{:T(128)} %clamp.3, (s32[16]{0:T(128)S(1)}, s32[16,16]{1,0:T(8,128)S(1)}, s32[16,16]{1,0:T(8,128)S(1)}, s32[16]{0:T(128)S(1)}, bf16[16,2,3,1,64,128]{5,4,3,2,1,0:T(8,128)(2,1)S(1)}, /*index=5*/s32[8,8,2]{1,2,0:T(2,128)S(1)}, ...), branch_computations={%region_4.9_spmd, %region_9.14_spmd, %region_14.19_spmd, %region_1... | conditional | flops 3012 | bytes 7104702 | solution.py:301
  6.9 0.1 fusion.9
  7.0 0.1 select_reduce_fusion.4
  7.2 0.1 select_reduce_fusion.5
  7.3 0.1 reshape.89.place_ref
  7.4 0.1 copy.46.index_ref
  7.5 1.7 %gather_fusion.2 = bf16[12,2,3,64,128]{4,3,2,1,0:T(8,128)(2,1)} fusion(bf16[16,2,3,64,128]{4,3,2,1,0:T(8,128)(2,1)S(1)} %bitcast.38, s32[1024]{0:T(1024)S(1)} %pad_clamp_fusion.2), kind=kCustom, calls=%fused_computation.2 | custom fusion | bytes 2359344 | tf_op jit(solution)/shard_map/cond/branch_2_fun/jit(_take)/gather | solution.py:287
  9.2 2.5 %copy.40 = bf16[6,2,2,3,64,128]{5,1,2,4,3,0:T(2,128)(2,1)S(1)} copy(bf16[6,2,2,3,64,128]{5,4,3,2,1,0:T(8,128)(2,1)} %bitcast.41) | data formatting | bytes 2359296 | tf_op jit(solution)/shard_map/cond/branch_2_fun/reshape | solution.py:292
  11.7 0.5 pad.14.h_ref
  12.2 98.5 %branch_2_fun.1 = f32[8,8,16,128]{3,2,1,0:T(8,128)S(1)} custom-call(s32[8,2]{1,0:T(8,128)S(1)} %reshape.89.place_ref, s32[8,8,2]{2,1,0:T(8,128)S(1)} %copy.46.index_ref, s32[8,8]{1,0:T(8,128)S(1)} %get-tuple-element.153.count_ref, bf16[6,3,65,4,128]{4,3,2,1,0:T(4,128)(2,1)S(1)} %pad.14.h_ref, bf16[8,3,256,128]{3,2,1,0:T(8,128)(2,1)S(1)} %get-tuple-element.156.tx_ref, ...), custom_call_target="tpu_custom_call" | custom-call | tf_op jit(solution)/shard_map/cond/branch_2_fun/pallas_call | solution.py:234
  111.3 1.0 copy.48
  (4 shorter events, 0.0 us)
Async XLA Ops:
  4.0 2.6 %copy-start = (bf16[16,2,3,1,64,128]{5,4,3,2,1,0:T(8,128)(2,1)S(1)}, bf16[16,2,3,1,64,128]{5,4,3,2,1,0:T(8,128)(2,1)}, u32[]{:S(2)}) copy-start(bf16[16,2,3,1,64,128]{5,4,3,2,1,0:T(8,128)(2,1)} %param.10) | copy-start | bytes 4718596
  4.0 2.6 %copy-start.1 = (f32[64,1,128]{2,1,0:T(1,128)S(1)}, f32[64,1,128]{2,1,0:T(1,128)}, u32[]{:S(2)}) copy-start(f32[64,1,128]{2,1,0:T(1,128)} %param.11) | copy-start | bytes 98308
  4.0 2.6 %copy-start.2 = (s32[8,8,2]{1,2,0:T(2,128)S(1)}, s32[8,8,2]{1,2,0:T(2,128)}, u32[]{:S(2)}) copy-start(s32[8,8,2]{1,2,0:T(2,128)} %param.14) | copy-start | bytes 1540
  4.1 2.6 %copy-start.3 = (f32[16,128]{1,0:T(8,128)S(1)}, f32[16,128]{1,0:T(8,128)}, u32[]{:S(2)}) copy-start(f32[16,128]{1,0:T(8,128)} %param.13) | copy-start | bytes 24580
  4.1 2.6 %copy-start.4 = (s32[8,8]{1,0:T(8,128)S(1)}, s32[8,8]{1,0:T(8,128)}, u32[]{:S(2)}) copy-start(s32[8,8]{1,0:T(8,128)} %param.15) | copy-start | bytes 772
